TPU v7x, 128 devices: a whole 4x4x4 slice. The times are simulated.
128 devices in a mesh: dp: 32 (over z, y, core), mp: 4 (over x).
Axes of the slice: x: 4, y: 4, z: 4, core: 2. Of those that a mesh axis runs over, the one named last changes fastest.
Arguments:
- features: bfloat16 [98304, 1024], P('dp'), may hold values from -6 to 6
- curvature: bfloat16 [98304, 4096], P('dp', 'mp'), may hold values from 0.099609375 to 2
- task_grad: float32 [1024, 4096], P('dp', 'mp'), may hold values from -6 to 6
Outputs:
- solution: float32 [1024, 4096], P('dp', 'mp')
- residual: float32 [1024, 4096], P('dp', 'mp')
All inputs are finite; a program needn't handle non-finite values.
Results may differ from a plain program's by a relative error of at most 0.0095.
The roundings to bfloat16 on the way count: a program that leaves them out, or rounds other values in their place, can miss the bound.
Values may be sent and summed in bfloat16 or wider, within the bound.
A program may use at most 64 MiB of HBM per device.

v0:
```python
import jax
import jax.numpy as jnp
from jax import lax
from jax.sharding import PartitionSpec as P

ITERS = 2
damp_coef = 0.5


def weigh_rows(curvature, projected):
    return (curvature * projected).astype(jnp.bfloat16)


def shards(features, curvature, task_grad):
    token_count = features.shape[0] * lax.axis_size("dp")

    def global_sums(values):
        return lax.psum(values, ("dp", "mp"))

    solution = jnp.zeros_like(task_grad)
    residual = task_grad
    direction = task_grad
    norm_now = jnp.sum(residual * residual)
    for turn in range(ITERS):
        dir_bf = direction.astype(jnp.bfloat16)
        gathered = lax.all_gather(dir_bf, "dp", axis=0, tiled=True)
        projected = jnp.dot(features, gathered, preferred_element_type=jnp.float32)
        weighted = weigh_rows(curvature, projected)
        summed = lax.psum_scatter(
            lax.dot_general(
                features, weighted, (((0,), (0,)), ((), ())), preferred_element_type=jnp.float32
            ),
            "dp",
            scatter_dimension=0,
            tiled=True,
        )
        curved = summed / token_count + damp_coef * direction
        pdot_local = jnp.sum(direction * curved)
        if turn == 0:
            norm_now, curv_dot = global_sums((norm_now, pdot_local))
        else:
            curv_dot = global_sums(pdot_local)
        step_len = norm_now / curv_dot
        solution = solution + step_len * direction
        residual = residual - step_len * curved
        if turn + 1 < ITERS:
            norm_next = global_sums(jnp.sum(residual * residual))
        if turn + 1 < ITERS:
            direction = residual + norm_next / norm_now * direction
            norm_now = norm_next
    return (solution, residual)


def solution(mesh):
    placed = (P("dp", None), P("dp", "mp"), P("dp", "mp"))
    return jax.shard_map(
        shards,
        mesh=mesh,
        in_specs=placed,
        out_specs=(P("dp", "mp"), P("dp", "mp")),
        check_vma=False,
    )
```

profile of v0, /device:TPU:1, one launch (start us, length us, event | category | flops | bytes accessed | tf_op | source)
XLA Modules:
  0.0 527.6 jit_solution(15309340547715633252)
XLA Ops:
  7.2 0.0 all-gather.3.cloned.1.call-start
  7.2 1.5 convert_element_type.17
  8.8 0.0 all-gather.3.cloned.1.call-update
  8.8 0.0 reduce-scatter.7.cloned.1.call-start
  8.8 49.4 %all-gather.3.cloned.1.call-done = bf16[1024,1024]{1,0:T(8,128)(2,1)} async-done(((bf16[32,1024]{1,0:T(8,128)(2,1)}), bf16[1024,1024]{1,0:T(8,128)(2,1)}) %all-gather.3.cloned.1.call-update) | async-done | bytes 2097168 | tf_op jit(solution)/shard_map/all_gather | solution.py:26
  58.2 22.5 %fusion.4 = f32[1024,1024]{0,1:T(8,128)} fusion(bf16[3072,1024]{1,0:T(8,128)(2,1)} %param.3, bf16[3072,1024]{1,0:T(8,128)(2,1)} %param.4, bf16[1024,1024]{1,0:T(8,128)(2,1)} %all-gather.3.cloned.1.call-done), kind=kOutput, calls=%fused_computation.6 | convolution fusion | flops 12894339072 | bytes 18874368 | tf_op jit(solution)/shard_map/dot_general | solution.py:30
  80.7 0.0 copy-start
  80.7 5.4 %copy.24 = f32[1024,1024]{1,0:T(8,128)} copy(f32[1024,1024]{0,1:T(8,128)} %fusion.4) | data formatting | bytes 8388608
  86.0 0.0 reduce-scatter.7.cloned.1.call-update
  86.1 0.0 all-gather.5.cloned.1.call-start
  86.1 79.7 %reduce-scatter.7.cloned.1.call-done = f32[32,1024]{1,0:T(8,128)} async-done(((f32[1024,1024]{1,0:T(8,128)}), f32[32,1024]{1,0:T(8,128)}) %reduce-scatter.7.cloned.1.call-update) | async-done | bytes 131088 | tf_op jit(solution)/shard_map/reduce_scatter | solution.py:29
  165.8 0.0 copy-done
  165.8 1.5 multiply_reduce_fusion.2
  167.4 65.9 %all-reduce = (f32[]{:T(128)}, f32[]{:T(128)}) all-reduce(f32[]{:T(128)} %get-tuple-element.7, f32[]{:T(128)} %get-tuple-element.6), channel_id=1, replica_groups=mesh['dp'=32,'mp'=4] {'dp','mp'}, use_global_device_ids=true, to_apply=%region_1.0 | all-reduce | flops 2 | bytes 16 | tf_op jit(solution)/shard_map/psum | solution.py:18
  234.7 1.5 multiply_reduce_fusion.1
  236.2 62.5 %psum.30 = f32[]{:T(128)} all-reduce(f32[]{:T(128)} %multiply_reduce_fusion.1), channel_id=1, replica_groups=mesh['dp'=32,'mp'=4] {'dp','mp'}, use_global_device_ids=true, to_apply=%region_6.0 | all-reduce | flops 1 | bytes 8 | tf_op jit(solution)/shard_map/psum | solution.py:18
  300.1 1.6 fusion.6
  301.7 0.0 all-gather.5.cloned.1.call-update
  301.7 0.0 reduce-scatter.9.cloned.1.call-start
  301.8 41.3 %all-gather.5.cloned.1.call-done = bf16[1024,1024]{1,0:T(8,128)(2,1)} async-done(((bf16[32,1024]{1,0:T(8,128)(2,1)}), bf16[1024,1024]{1,0:T(8,128)(2,1)}) %all-gather.5.cloned.1.call-update) | async-done | bytes 2097168 | tf_op jit(solution)/shard_map/all_gather | solution.py:26
  343.1 22.3 %fusion.5 = f32[1024,1024]{0,1:T(8,128)} fusion(bf16[3072,1024]{1,0:T(8,128)(2,1)} %param.3, bf16[3072,1024]{1,0:T(8,128)(2,1)} %param.4, bf16[1024,1024]{1,0:T(8,128)(2,1)} %all-gather.5.cloned.1.call-done), kind=kOutput, calls=%fused_computation.7 | convolution fusion | flops 12894339072 | bytes 18874368 | tf_op jit(solution)/shard_map/dot_general | solution.py:30
  365.3 0.0 copy-start.1
  365.4 5.4 %copy.26 = f32[1024,1024]{1,0:T(8,128)} copy(f32[1024,1024]{0,1:T(8,128)} %fusion.5) | data formatting | bytes 8388608
  370.7 0.0 reduce-scatter.9.cloned.1.call-update
  370.8 79.8 %reduce-scatter.9.cloned.1.call-done = f32[32,1024]{1,0:T(8,128)} async-done(((f32[1024,1024]{1,0:T(8,128)}), f32[32,1024]{1,0:T(8,128)}) %reduce-scatter.9.cloned.1.call-update) | async-done | bytes 131088 | tf_op jit(solution)/shard_map/reduce_scatter | solution.py:29
  450.5 0.0 copy-done.1
  450.5 1.6 multiply_reduce_fusion
  452.1 65.9 %psum.31 = f32[]{:T(128)} all-reduce(f32[]{:T(128)} %multiply_reduce_fusion), channel_id=1, replica_groups=mesh['dp'=32,'mp'=4] {'dp','mp'}, use_global_device_ids=true, to_apply=%region_9.0 | all-reduce | flops 1 | bytes 8 | tf_op jit(solution)/shard_map/psum | solution.py:18
  519.4 1.7 multiply_subtract_fusion
Async XLA Ops:
  7.2 51.0 %all-gather.3.cloned.1.call-start = ((), (), s32[]{:S(2)}) async-start(), calls=%async_computation.2 | async-start | bytes 2162688 | tf_op jit(solution)/shard_map/all_gather | solution.py:26
  8.8 157.1 %reduce-scatter.7.cloned.1.call-start = ((), (), s32[]{:S(2)}) async-start(), calls=%async_computation.4 | async-start | bytes 4325376 | tf_op jit(solution)/shard_map/reduce_scatter | solution.py:29
  80.7 85.2 %copy-start = (f32[32,1024]{1,0:T(8,128)S(1)}, f32[32,1024]{1,0:T(8,128)}, u32[]{:S(2)}) copy-start(f32[32,1024]{1,0:T(8,128)} %param.5) | copy-start | bytes 393220
  86.1 257.0 %all-gather.5.cloned.1.call-start = ((), (), s32[]{:S(2)}) async-start(), calls=%async_computation.3 | async-start | bytes 2162688 | tf_op jit(solution)/shard_map/all_gather | solution.py:26
  301.7 148.8 %reduce-scatter.9.cloned.1.call-start = ((), (), s32[]{:S(2)}) async-start(), calls=%async_computation.5 | async-start | bytes 4325376 | tf_op jit(solution)/shard_map/reduce_scatter | solution.py:29
  365.3 85.2 %copy-start.1 = (f32[32,1024]{1,0:T(8,128)S(1)}, f32[32,1024]{1,0:T(8,128)}, u32[]{:S(2)}) copy-start(f32[32,1024]{1,0:T(8,128)} %reduce-scatter.7.cloned.1.call-done) | copy-start | bytes 393220
Sparse Core Ops, SparseCore 0:
  10.8 47.3 all-gather.2
  86.2 79.5 reduce-scatter.6
  301.8 41.2 all-gather.4
  370.9 79.6 reduce-scatter.8
where the time goes:
time: 528 us
  waiting for transfers between devices  250 us (47%)
  blocking collectives  194 us (37%)
  matrix products  44.8 us (8%)
  between operations  17.8 us (3%)
  local copies, waits for them, and re-layouts  10.8 us (2%)
  other arithmetic  9.45 us (2%)
    psum x3, blocking collectives, global_sums(): return lax.psum(values, ('dp', 'mp'))  194 us
    reduce_scatter x2, waiting for transfers between devices, shards(): lax.psum_scatter(lax.dot_general(features, weighted, (((0,), (0,)), ((),...  160 us
    all_gather x2, waiting for transfers between devices, shards(): gathered = lax.all_gather(dir_bf, 'dp', axis=0, tiled=True)  90.7 us
    dot_general x2, matrix products, shards(): lax.dot_general(features, weighted, (((0,), (0,)), ((), ())), preferred_e...  44.8 us
    unnamed x6, local copies, waits for them, and re-layouts  10.8 us
  transfers between devices with their start and end apart: 4, of which 4 were waited for; matrix products, arithmetic and copies ran while one was open for 0% of the time, Pallas kernels for 0%

commit v1 on v0

--- a/solution.py
+++ b/solution.py
@@ -15,7 +15,7 @@
     token_count = features.shape[0] * lax.axis_size("dp")
 
     def global_sums(values):
-        return lax.psum(values, ("dp", "mp"))
+        return lax.psum(lax.psum(values, "dp"), "mp")
 
     solution = jnp.zeros_like(task_grad)
     residual = task_grad

time: 528 us -> 556 us (1.053)
  blocking collectives: 194 us -> 220 us
    psum x3 -> x6, blocking collectives: 194 us -> 220 us  [global_sums(): return lax.psum(lax.psum(values, 'dp'), 'mp')]
where the time goes in v1:
time: 556 us; the launch traced here: 553 us
  waiting for transfers between devices  250 us (45%)
  blocking collectives  220 us (40%)
  matrix products  44.6 us (8%)
  between operations  17.8 us (3%)
  local copies, waits for them, and re-layouts  10.8 us (2%)
  other arithmetic  9.45 us (2%)
    psum x6, blocking collectives, global_sums(): return lax.psum(lax.psum(values, 'dp'), 'mp')  220 us
    reduce_scatter x2, waiting for transfers between devices, shards(): lax.psum_scatter(lax.dot_general(features, weighted, (((0,), (0,)), ((),...  159 us
    all_gather x2, waiting for transfers between devices, shards(): gathered = lax.all_gather(dir_bf, 'dp', axis=0, tiled=True)  90.4 us
    dot_general x2, matrix products, shards(): lax.dot_general(features, weighted, (((0,), (0,)), ((), ())), preferred_e...  44.6 us
  transfers between devices with their start and end apart: 4, of which 4 were waited for; matrix products, arithmetic and copies ran while one was open for 0% of the time, Pallas kernels for 0%

profile of v1, /device:TPU:1, one launch (start us, length us, event | category | flops | bytes accessed | tf_op | source)
XLA Modules:
  0.0 553.3 jit_solution(665560802573850543)
XLA Ops:
  7.2 0.0 all-gather.3.cloned.1.call-start
  7.2 1.5 convert_element_type.17
  8.8 0.0 all-gather.3.cloned.1.call-update
  8.8 0.0 reduce-scatter.7.cloned.1.call-start
  8.8 49.4 %all-gather.3.cloned.1.call-done = bf16[1024,1024]{1,0:T(8,128)(2,1)} async-done(((bf16[32,1024]{1,0:T(8,128)(2,1)}), bf16[1024,1024]{1,0:T(8,128)(2,1)}) %all-gather.3.cloned.1.call-update) | async-done | bytes 2097168 | tf_op jit(solution)/shard_map/all_gather | solution.py:26
  58.2 22.3 %fusion.4 = f32[1024,1024]{0,1:T(8,128)} fusion(bf16[3072,1024]{1,0:T(8,128)(2,1)} %param.3, bf16[3072,1024]{1,0:T(8,128)(2,1)} %param.4, bf16[1024,1024]{1,0:T(8,128)(2,1)} %all-gather.3.cloned.1.call-done), kind=kOutput, calls=%fused_computation.6 | convolution fusion | flops 12894339072 | bytes 18874368 | tf_op jit(solution)/shard_map/dot_general | solution.py:30
  80.5 0.0 copy-start
  80.5 5.4 copy.24
  85.8 0.0 reduce-scatter.7.cloned.1.call-update
  85.9 0.0 all-gather.5.cloned.1.call-start
  85.9 79.7 %reduce-scatter.7.cloned.1.call-done = f32[32,1024]{1,0:T(8,128)} async-done(((f32[1024,1024]{1,0:T(8,128)}), f32[32,1024]{1,0:T(8,128)}) %reduce-scatter.7.cloned.1.call-update) | async-done | bytes 131088 | tf_op jit(solution)/shard_map/reduce_scatter | solution.py:29
  165.6 0.0 copy-done
  165.6 1.5 multiply_reduce_fusion.2
  167.2 65.0 %all-reduce = (f32[]{:T(128)}, f32[]{:T(128)}) all-reduce(f32[]{:T(128)} %get-tuple-element.7, f32[]{:T(128)} %get-tuple-element.6), channel_id=1, replica_groups=mesh['dp'=32,'mp'=4] {'dp'}, use_global_device_ids=true, to_apply=%region_1.0 | all-reduce | flops 2 | bytes 16 | tf_op jit(solution)/shard_map/psum | solution.py:18
  232.2 9.0 %all-reduce.1 = (f32[]{:T(128)}, f32[]{:T(128)}) all-reduce(f32[]{:T(128)} %get-tuple-element.8, f32[]{:T(128)} %get-tuple-element.9), channel_id=1, replica_groups=mesh['dp'=32,'mp'=4] {'mp'}, use_global_device_ids=true, to_apply=%region_2.0 | all-reduce | flops 2 | bytes 16 | tf_op jit(solution)/shard_map/psum | solution.py:18
  242.6 1.5 multiply_reduce_fusion.1
  244.1 65.7 %psum.60 = f32[]{:T(128)} all-reduce(f32[]{:T(128)} %multiply_reduce_fusion.1), channel_id=1, replica_groups=mesh['dp'=32,'mp'=4] {'dp'}, use_global_device_ids=true, to_apply=%region_8.0 | all-reduce | flops 1 | bytes 8 | tf_op jit(solution)/shard_map/psum | solution.py:18
  309.8 6.7 %psum.61 = f32[]{:T(128)} all-reduce(f32[]{:T(128)} %psum.60), channel_id=1, replica_groups=mesh['dp'=32,'mp'=4] {'mp'}, use_global_device_ids=true, to_apply=%region_9.0 | all-reduce | flops 1 | bytes 8 | tf_op jit(solution)/shard_map/psum | solution.py:18
  317.8 1.6 fusion.6
  319.4 0.0 all-gather.5.cloned.1.call-update
  319.4 0.2 reduce-scatter.9.cloned.1.call-start
  319.7 41.0 %all-gather.5.cloned.1.call-done = bf16[1024,1024]{1,0:T(8,128)(2,1)} async-done(((bf16[32,1024]{1,0:T(8,128)(2,1)}), bf16[1024,1024]{1,0:T(8,128)(2,1)}) %all-gather.5.cloned.1.call-update) | async-done | bytes 2097168 | tf_op jit(solution)/shard_map/all_gather | solution.py:26
  360.7 22.3 %fusion.5 = f32[1024,1024]{0,1:T(8,128)} fusion(bf16[3072,1024]{1,0:T(8,128)(2,1)} %param.3, bf16[3072,1024]{1,0:T(8,128)(2,1)} %param.4, bf16[1024,1024]{1,0:T(8,128)(2,1)} %all-gather.5.cloned.1.call-done), kind=kOutput, calls=%fused_computation.7 | convolution fusion | flops 12894339072 | bytes 18874368 | tf_op jit(solution)/shard_map/dot_general | solution.py:30
  383.0 0.0 copy-start.1
  383.0 5.4 copy.26
  388.4 0.0 reduce-scatter.9.cloned.1.call-update
  388.4 79.8 %reduce-scatter.9.cloned.1.call-done = f32[32,1024]{1,0:T(8,128)} async-done(((f32[1024,1024]{1,0:T(8,128)}), f32[32,1024]{1,0:T(8,128)}) %reduce-scatter.9.cloned.1.call-update) | async-done | bytes 131088 | tf_op jit(solution)/shard_map/reduce_scatter | solution.py:29
  468.2 0.0 copy-done.1
  468.2 1.6 multiply_reduce_fusion
  469.7 65.0 %psum.62 = f32[]{:T(128)} all-reduce(f32[]{:T(128)} %multiply_reduce_fusion), channel_id=1, replica_groups=mesh['dp'=32,'mp'=4] {'dp'}, use_global_device_ids=true, to_apply=%region_12.0 | all-reduce | flops 1 | bytes 8 | tf_op jit(solution)/shard_map/psum | solution.py:18
  534.8 9.0 %psum.63 = f32[]{:T(128)} all-reduce(f32[]{:T(128)} %psum.62), channel_id=1, replica_groups=mesh['dp'=32,'mp'=4] {'mp'}, use_global_device_ids=true, to_apply=%region_13.0 | all-reduce | flops 1 | bytes 8 | tf_op jit(solution)/shard_map/psum | solution.py:18
  545.1 1.7 multiply_subtract_fusion
Async XLA Ops:
  7.2 51.0 %all-gather.3.cloned.1.call-start = ((), (), s32[]{:S(2)}) async-start(), calls=%async_computation.2 | async-start | bytes 2162688 | tf_op jit(solution)/shard_map/all_gather | solution.py:26
  8.8 156.8 %reduce-scatter.7.cloned.1.call-start = ((), (), s32[]{:S(2)}) async-start(), calls=%async_computation.4 | async-start | bytes 4325376 | tf_op jit(solution)/shard_map/reduce_scatter | solution.py:29
  80.5 85.2 %copy-start = (f32[32,1024]{1,0:T(8,128)S(1)}, f32[32,1024]{1,0:T(8,128)}, u32[]{:S(2)}) copy-start(f32[32,1024]{1,0:T(8,128)} %param.5) | copy-start | bytes 393220
  85.9 274.9 %all-gather.5.cloned.1.call-start = ((), (), s32[]{:S(2)}) async-start(), calls=%async_computation.3 | async-start | bytes 2162688 | tf_op jit(solution)/shard_map/all_gather | solution.py:26
  319.4 148.7 %reduce-scatter.9.cloned.1.call-start = ((), (), s32[]{:S(2)}) async-start(), calls=%async_computation.5 | async-start | bytes 4325376 | tf_op jit(solution)/shard_map/reduce_scatter | solution.py:29
  383.0 85.2 %copy-start.1 = (f32[32,1024]{1,0:T(8,128)S(1)}, f32[32,1024]{1,0:T(8,128)}, u32[]{:S(2)}) copy-start(f32[32,1024]{1,0:T(8,128)} %reduce-scatter.7.cloned.1.call-done) | copy-start | bytes 393220
Sparse Core Ops, SparseCore 0:
  10.8 47.3 all-gather.2
  86.0 79.5 reduce-scatter.6
  319.6 41.1 all-gather.4
  388.5 79.5 reduce-scatter.8

commit v2 on v0

--- a/solution.py
+++ b/solution.py
@@ -23,7 +23,9 @@
     norm_now = jnp.sum(residual * residual)
     for turn in range(ITERS):
         dir_bf = direction.astype(jnp.bfloat16)
-        gathered = lax.all_gather(dir_bf, "dp", axis=0, tiled=True)
+        gathered = jnp.concatenate(
+            lax.all_to_all(jnp.stack([dir_bf] * lax.axis_size("dp")), "dp", 0, 0), axis=0
+        )
         projected = jnp.dot(features, gathered, preferred_element_type=jnp.float32)
         weighted = weigh_rows(curvature, projected)
         summed = lax.psum_scatter(

time: 528 us -> 503 us (0.953)
  waiting for transfers between devices: 250 us -> 155 us
  blocking collectives: 194 us -> 265 us
    all_gather x2 -> x0, waiting for transfers between devices: 90.7 us -> none  [shards(): gathered = lax.all_gather(dir_bf, 'dp', axis=0, tiled=True)]
    all_to_all x0 -> x2, blocking collectives: none -> 71.1 us  [shards(): lax.all_to_all(jnp.stack([dir_bf] * lax.axis_size('dp')), 'dp', 0, 0)]
  transfers between devices with their start and end apart: 4 -> 2, of which waited for: 4 -> 2; matrix products, arithmetic and copies ran while one was open for 0% -> 0% of each run, Pallas kernels for 0% -> 0%
where the time goes in v2:
time: 503 us; the launch traced here: 502 us
  blocking collectives  265 us (53%)
  waiting for transfers between devices  155 us (31%)
  matrix products  43.6 us (9%)
  between operations  18.1 us (4%)
  local copies, waits for them, and re-layouts  11.3 us (2%)
  other arithmetic  8.19 us (2%)
    psum x3, blocking collectives, global_sums(): return lax.psum(values, ('dp', 'mp'))  194 us
    reduce_scatter x2, waiting for transfers between devices, shards(): lax.psum_scatter(lax.dot_general(features, weighted, (((0,), (0,)), ((),...  155 us
    all_to_all x2, blocking collectives, shards(): lax.all_to_all(jnp.stack([dir_bf] * lax.axis_size('dp')), 'dp', 0, 0)  71.1 us
    dot_general x2, matrix products, shards(): lax.dot_general(features, weighted, (((0,), (0,)), ((), ())), preferred_e...  43.6 us
    unnamed x6, local copies, waits for them, and re-layouts  10.8 us
  transfers between devices with their start and end apart: 2, of which 2 were waited for; matrix products, arithmetic and copies ran while one was open for 0% of the time, Pallas kernels for 0%

profile of v2, /device:TPU:1, one launch (start us, length us, event | category | flops | bytes accessed | tf_op | source)
XLA Modules:
  0.0 501.8 jit_solution(7328540066211113691)
XLA Ops:
  7.2 0.0 reduce-scatter.7.cloned.1.call-start
  7.2 0.9 convert_element_type.17
  8.1 0.2 stack.4
  8.4 37.7 %all_to_all.10 = bf16[32,32,1024]{2,1,0:T(8,128)(2,1)S(1)} all-to-all(bf16[32,32,1024]{2,1,0:T(8,128)(2,1)S(1)} %stack.4), channel_id=1, replica_groups=mesh['dp'=32,'mp'=4] {'dp'}, dimensions={0} | all-to-all | bytes 4194304 | tf_op jit(solution)/shard_map/all_to_all | solution.py:27
  46.1 21.9 %fusion.4 = f32[1024,1024]{0,1:T(8,128)} fusion(bf16[3072,1024]{1,0:T(8,128)(2,1)} %param.3, bf16[3072,1024]{1,0:T(8,128)(2,1)} %param.4, bf16[1024,1024]{1,0:T(8,128)(2,1)S(1)} %bitcast.20), kind=kOutput, calls=%fused_computation.6 | convolution fusion | flops 12894339072 | bytes 18874368 | tf_op jit(solution)/shard_map/dot_general | solution.py:32
  68.0 0.0 copy-start
  68.0 5.4 %copy.25 = f32[1024,1024]{1,0:T(8,128)} copy(f32[1024,1024]{0,1:T(8,128)} %fusion.4) | data formatting | bytes 8388608
  73.4 0.0 reduce-scatter.7.cloned.1.call-update
  73.4 0.0 reduce-scatter.9.cloned.1.call-start
  73.4 78.5 %reduce-scatter.7.cloned.1.call-done = f32[32,1024]{1,0:T(8,128)} async-done(((f32[1024,1024]{1,0:T(8,128)}), f32[32,1024]{1,0:T(8,128)}) %reduce-scatter.7.cloned.1.call-update) | async-done | bytes 131088 | tf_op jit(solution)/shard_map/reduce_scatter | solution.py:31
  151.9 0.0 copy-done
  151.9 1.5 multiply_reduce_fusion.2
  153.4 65.9 %all-reduce = (f32[]{:T(128)}, f32[]{:T(128)}) all-reduce(f32[]{:T(128)} %get-tuple-element.7, f32[]{:T(128)} %get-tuple-element.6), channel_id=1, replica_groups=mesh['dp'=32,'mp'=4] {'dp','mp'}, use_global_device_ids=true, to_apply=%region_1.0 | all-reduce | flops 2 | bytes 16 | tf_op jit(solution)/shard_map/psum | solution.py:18
  220.7 1.5 multiply_reduce_fusion.1
  222.2 62.5 %psum.30 = f32[]{:T(128)} all-reduce(f32[]{:T(128)} %multiply_reduce_fusion.1), channel_id=1, replica_groups=mesh['dp'=32,'mp'=4] {'dp','mp'}, use_global_device_ids=true, to_apply=%region_6.0 | all-reduce | flops 1 | bytes 8 | tf_op jit(solution)/shard_map/psum | solution.py:18
  286.1 0.9 fusion.6
  287.0 0.2 stack.5
  287.3 33.4 %all_to_all.11 = bf16[32,32,1024]{2,1,0:T(8,128)(2,1)S(1)} all-to-all(bf16[32,32,1024]{2,1,0:T(8,128)(2,1)S(1)} %stack.5), channel_id=1, replica_groups=mesh['dp'=32,'mp'=4] {'dp'}, dimensions={0} | all-to-all | bytes 4194304 | tf_op jit(solution)/shard_map/all_to_all | solution.py:27
  320.7 21.7 %fusion.5 = f32[1024,1024]{0,1:T(8,128)} fusion(bf16[3072,1024]{1,0:T(8,128)(2,1)} %param.3, bf16[3072,1024]{1,0:T(8,128)(2,1)} %param.4, bf16[1024,1024]{1,0:T(8,128)(2,1)S(1)} %bitcast.21), kind=kOutput, calls=%fused_computation.7 | convolution fusion | flops 12894339072 | bytes 18874368 | tf_op jit(solution)/shard_map/dot_general | solution.py:32
  342.4 0.0 copy-start.1
  342.5 5.4 %copy.27 = f32[1024,1024]{1,0:T(8,128)} copy(f32[1024,1024]{0,1:T(8,128)} %fusion.5) | data formatting | bytes 8388608
  347.8 0.0 reduce-scatter.9.cloned.1.call-update
  347.9 76.6 %reduce-scatter.9.cloned.1.call-done = f32[32,1024]{1,0:T(8,128)} async-done(((f32[1024,1024]{1,0:T(8,128)}), f32[32,1024]{1,0:T(8,128)}) %reduce-scatter.9.cloned.1.call-update) | async-done | bytes 131088 | tf_op jit(solution)/shard_map/reduce_scatter | solution.py:31
  424.5 0.0 copy-done.1
  424.5 1.6 multiply_reduce_fusion
  426.1 65.9 %psum.31 = f32[]{:T(128)} all-reduce(f32[]{:T(128)} %multiply_reduce_fusion), channel_id=1, replica_groups=mesh['dp'=32,'mp'=4] {'dp','mp'}, use_global_device_ids=true, to_apply=%region_9.0 | all-reduce | flops 1 | bytes 8 | tf_op jit(solution)/shard_map/psum | solution.py:18
  493.3 1.7 multiply_subtract_fusion
Async XLA Ops:
  7.2 144.7 %reduce-scatter.7.cloned.1.call-start = ((), (), s32[]{:S(2)}) async-start(), calls=%async_computation.4 | async-start | bytes 4325376 | tf_op jit(solution)/shard_map/reduce_scatter | solution.py:31
  68.0 83.9 %copy-start = (f32[32,1024]{1,0:T(8,128)S(1)}, f32[32,1024]{1,0:T(8,128)}, u32[]{:S(2)}) copy-start(f32[32,1024]{1,0:T(8,128)} %param.5) | copy-start | bytes 393220
  73.4 351.1 %reduce-scatter.9.cloned.1.call-start = ((), (), s32[]{:S(2)}) async-start(), calls=%async_computation.5 | async-start | bytes 4325376 | tf_op jit(solution)/shard_map/reduce_scatter | solution.py:31
  342.4 82.0 %copy-start.1 = (f32[32,1024]{1,0:T(8,128)S(1)}, f32[32,1024]{1,0:T(8,128)}, u32[]{:S(2)}) copy-start(f32[32,1024]{1,0:T(8,128)} %reduce-scatter.7.cloned.1.call-done) | copy-start | bytes 393220
Sparse Core Ops, SparseCore 0:
  73.5 78.3 reduce-scatter.6
  348.0 76.4 reduce-scatter.8
